TPU v7x, 256 devices: a whole 4x4x8 slice. The times are simulated.
256 devices in a mesh: seq: 64 (over z, y, core), tensor: 4 (over x).
Axes of the slice: x: 4, y: 4, z: 8, core: 2. Of those that a mesh axis runs over, the one named last changes fastest.
Arguments:
- tokens: bfloat16 [32768, 2048], P('seq', 'tensor')
- norm_gain: float32 [2048], replicated, may hold values from 0.5 to 1.5
- w_qkv: bfloat16 [2048, 4, 1024], P(None, 'tensor'), may hold values from -0.125 to 0.125
- w_gate_out: bfloat16 [2048, 2048], P(None, 'tensor'), may hold values from -0.125 to 0.125
- gate_down: bfloat16 [2048, 16], replicated
- gate_up: float32 [16, 4, 256], P(None, 'tensor')
- gate_bias: float32 [4, 256], P('tensor')
- conv_weight: float32 [4, 4, 1024], P(None, 'tensor'), may hold values from -3 to 3
- head_gain: float32 [512], replicated, may hold values from 0.5 to 1.5
- w_out: bfloat16 [2048, 2048], P('tensor'), may hold values from -0.125 to 0.125
- spans: int32 [3], replicated, may hold values from 1 to 48, 64 in all
- fills: int32 [3], replicated, may hold values from 1 to 512
- request_prompt: int32 [128], P('seq'), may hold values from -1 to 2, as said below
Outputs:
- mixed: bfloat16 [32768, 2048], P(('seq', 'tensor'))
- owner_state: float32 [128, 4, 256, 512], P('seq', 'tensor')
- owner_edge: bfloat16 [128, 3, 4, 1024], P('seq', None, 'tensor')
Inputs may be any that keep to these rules, and one draw needn't show every extreme that they name: `spans`: the prompts lie along seq in order and together cover all its indices. `request_prompt`: slots r * 2 to r * 2 + 1 belong to index r of seq; the first slot of every index names a prompt; every prompt is named by some slot.
All inputs are finite; a program needn't handle non-finite values.
Results may differ from a plain program's by a relative error of at most 0.0095.
Values may be sent and summed in bfloat16 or wider, within the bound.
A program may use at most 128 MiB of HBM per device.

v0:
```python
import jax
import jax.numpy as jnp
from jax import lax
from jax.sharding import PartitionSpec as P

STRETCH = 64
EPS_IN = 1e-06
EPS_HEAD = 1e-05
EXACT_MATMUL = lax.Precision.HIGHEST


def from_behind(array, axis, by):
    peers = lax.axis_size(axis)
    pairs = [(i, i + by) for i in range(peers) if 0 <= i + by < peers]
    return lax.ppermute(array, axis, pairs)


def broadcast(block, axis, source):
    block = jnp.where(lax.axis_index(axis) == source, block, jnp.zeros_like(block))
    return lax.psum(block, axis)


def block_pass(carry, pieces):
    passed_along_state, offset = carry
    q_blk, k_blk, value_block, decay_blk = pieces
    block_rows = q_blk.shape[0]
    k_wide = k_blk.astype(jnp.float32)
    cumulative = jnp.cumsum(decay_blk, axis=0)
    query_decayed = (q_blk * jnp.exp(cumulative)).astype(jnp.bfloat16)
    pair_decay = jnp.exp(jnp.minimum(cumulative[:, None] - cumulative[None, :], 0.0))
    causal_mask = jnp.arange(block_rows)[:, None] >= jnp.arange(block_rows)[None, :]
    scores = jnp.einsum("ihk,jhk,ijhk->hij", q_blk, k_wide, pair_decay, precision=EXACT_MATMUL)
    scores = jnp.where(causal_mask[None], scores, 0.0).astype(jnp.bfloat16)
    intra_term = jnp.einsum("hij,jhv->ihv", scores, value_block, preferred_element_type=jnp.float32)
    closing_decay = cumulative[-1]
    weight_applied = (k_wide * jnp.exp(closing_decay[None] - cumulative)).astype(jnp.bfloat16)
    updated = jnp.exp(closing_decay)[:, :, None] * passed_along_state + jnp.einsum(
        "qbr,qbp->brp", weight_applied, value_block, preferred_element_type=jnp.float32
    )
    return (
        (updated, offset + closing_decay),
        (intra_term, passed_along_state, offset, query_decayed),
    )


def body(
    tokens,
    norm_gain,
    w_qkv,
    w_gate_out,
    gate_down,
    gate_up,
    gate_bias,
    conv_weight,
    head_gain,
    w_out,
    spans,
    fills,
    request_prompt,
):
    row_count = tokens.shape[0]
    local_heads = w_qkv.shape[1]
    width_qkv = w_qkv.shape[2]
    key_width = gate_up.shape[2]
    value_width = head_gain.shape[0]
    model_width = norm_gain.shape[0]
    taps = conv_weight.shape[0]
    prompts = spans.shape[0]
    slot_count = request_prompt.shape[0]
    seq_index = lax.axis_index("seq")
    span_ends = jnp.cumsum(spans)
    starts = span_ends - spans
    my_prompt = jnp.sum((span_ends <= seq_index).astype(jnp.int32))
    picked = jnp.arange(prompts, dtype=jnp.int32) == my_prompt
    first_dev = jnp.sum(jnp.where(picked, starts, 0))
    last_dev = jnp.sum(jnp.where(picked, span_ends - 1, 0))
    is_start = seq_index == first_dev
    is_last = seq_index == last_dev
    live_rows = jnp.where(is_last, jnp.sum(jnp.where(picked, fills, 0)), row_count)
    valid = jnp.arange(row_count, dtype=jnp.int32) < live_rows
    value_entries = tokens.astype(jnp.float32)
    squares = lax.psum(jnp.sum(value_entries * value_entries, axis=1), "tensor")
    inverse = lax.rsqrt(squares / model_width + EPS_IN)
    flat_qkv = w_qkv.reshape(model_width, local_heads * width_qkv)
    normed = (
        lax.all_gather(tokens, "tensor", axis=1, tiled=True).astype(jnp.float32)
        * inverse[:, None]
        * norm_gain[None, :]
    ).astype(jnp.bfloat16)
    qkv_sum = jnp.dot(normed, flat_qkv, preferred_element_type=jnp.float32)
    gate_sum = jnp.dot(normed, w_gate_out, preferred_element_type=jnp.float32)
    low_rank = jnp.dot(normed, gate_down, preferred_element_type=jnp.float32)
    projected = qkv_sum.astype(jnp.bfloat16).reshape(row_count, local_heads, width_qkv)
    gate_rounded = lax.optimization_barrier(gate_sum.astype(jnp.bfloat16))
    gate_values = gate_rounded.astype(jnp.float32).reshape(row_count, local_heads, value_width)
    logits = jnp.dot(
        low_rank, gate_up.reshape(gate_up.shape[0], local_heads * key_width), precision=EXACT_MATMUL
    )
    logits = logits.reshape(row_count, local_heads, key_width) + gate_bias[None]
    log_decay = jnp.where(valid[:, None, None], jax.nn.log_sigmoid(logits) / 16.0, 0.0)
    tail_rows = projected[row_count - taps + 1 :]
    previous = from_behind(tail_rows, "seq", 1)
    previous = jnp.where(is_start, jnp.zeros_like(previous), previous)
    extended = jnp.concatenate([previous, projected], axis=0)
    conv_sum = jnp.zeros((row_count, local_heads, width_qkv), jnp.float32)
    for offset in range(taps):
        conv_sum = conv_sum + conv_weight[offset][None] * extended[
            offset : offset + row_count
        ].astype(jnp.float32)
    activated = jax.nn.silu(conv_sum).astype(jnp.bfloat16)
    query_rows = activated[:, :, :key_width].astype(jnp.float32) * key_width ** (-0.5)
    key_rows = jnp.where(
        valid[:, None, None],
        activated[:, :, key_width : 2 * key_width],
        jnp.zeros((), jnp.bfloat16),
    )
    value_rows = activated[:, :, 2 * key_width :]

    def into_blocks(array):
        return array.reshape(row_count // STRETCH, STRETCH, local_heads, array.shape[-1])

    start_carry = (
        jnp.zeros((local_heads, key_width, value_width), jnp.float32),
        jnp.zeros((local_heads, key_width), jnp.float32),
    )
    (local_state, decay_sum), (local_out, block_starts, block_offsets, query_decayed) = lax.scan(
        block_pass,
        start_carry,
        (
            into_blocks(query_rows),
            into_blocks(key_rows),
            into_blocks(value_rows),
            into_blocks(log_decay),
        ),
    )
    decay_total = jnp.exp(decay_sum)
    span_most = 3 * lax.axis_size("seq") // 4

    def relay(turn, carry):
        received, outgoing = carry
        received = from_behind(outgoing, "seq", 1)
        received = jnp.where(is_start, jnp.zeros_like(received), received)
        return (received, decay_total[:, :, None] * received + local_state)

    incoming, _ = lax.fori_loop(0, span_most - 1, relay, (jnp.zeros_like(local_state), local_state))
    full_starts = block_starts + jnp.exp(block_offsets)[:, :, :, None] * incoming[None]
    cross_block_term = jnp.einsum(
        "bchk,bhkv->bchv",
        query_decayed,
        full_starts.astype(jnp.bfloat16),
        preferred_element_type=jnp.float32,
    )
    attended = (cross_block_term + local_out).reshape(row_count, local_heads, value_width)
    end_state = decay_total[:, :, None] * incoming + local_state
    mean_square = jnp.mean(attended * attended, axis=2, keepdims=True)
    gated = (
        attended
        * lax.rsqrt(mean_square + EPS_HEAD)
        * head_gain[None, None, :]
        * jax.nn.silu(gate_values)
    ).astype(jnp.bfloat16)
    gated = gated.reshape(row_count, local_heads * value_width)
    share = row_count // lax.axis_size("tensor")
    summed = lax.psum_scatter(
        jnp.dot(gated, w_out, preferred_element_type=jnp.float32).astype(jnp.bfloat16),
        "tensor",
        scatter_dimension=0,
        tiled=True,
    ).astype(jnp.float32)
    own_rows = lax.axis_index("tensor") * share + jnp.arange(share, dtype=jnp.int32)
    mixed = jnp.where((own_rows < live_rows)[:, None], summed, 0.0).astype(jnp.bfloat16)
    edge_rows = lax.dynamic_slice_in_dim(extended, live_rows, taps - 1, 0)
    edge_wide = edge_rows.astype(jnp.float32)

    def deliver(turn, carry):
        states_sofar, edges_sofar = carry
        root = jnp.sum(jnp.where(jnp.arange(prompts, dtype=jnp.int32) == turn, span_ends - 1, 0))
        got_state, got_edge = (
            broadcast(end_state.astype(jnp.bfloat16), "seq", root).astype(end_state.dtype),
            broadcast(edge_wide.astype(jnp.bfloat16), "seq", root).astype(edge_wide.dtype),
        )
        wanted = (request_prompt == turn)[:, None, None, None]
        return (
            jnp.where(wanted, got_state[None], states_sofar),
            jnp.where(wanted, got_edge[None], edges_sofar),
        )

    empty = (
        jnp.zeros((slot_count, local_heads, key_width, value_width), jnp.float32),
        jnp.zeros((slot_count, taps - 1, local_heads, width_qkv), jnp.float32),
    )
    owner_state, owner_wide = lax.fori_loop(0, prompts, deliver, empty)
    owner_edge = owner_wide.astype(jnp.bfloat16)
    return (mixed, owner_state, owner_edge)


def solution(mesh):
    return jax.shard_map(
        body,
        mesh=mesh,
        in_specs=(
            P("seq", "tensor"),
            P(),
            P(None, "tensor", None),
            P(None, "tensor"),
            P(),
            P(None, "tensor", None),
            P("tensor", None),
            P(None, "tensor", None),
            P(),
            P("tensor", None),
            P(),
            P(),
            P("seq"),
        ),
        out_specs=(
            P(("seq", "tensor"), None),
            P("seq", "tensor", None, None),
            P("seq", None, "tensor", None),
        ),
        check_vma=False,
    )
```

profile of v0, /device:TPU:1, one launch (start us, length us, event | category | flops | bytes accessed | tf_op | source)
XLA Modules:
  0.0 1430.1 jit_solution(8142053873680387150)
XLA Ops:
  14.6 9.3 psum.35
  24.7 22.1 %all-gather.2.cloned.1.call-done = bf16[512,2048]{1,0:T(8,128)(2,1)} async-done(((bf16[512,512]{1,0:T(8,128)(2,1)}), bf16[512,2048]{1,0:T(8,128)(2,1)}) %all-gather.2.cloned.1.call-update) | async-done | bytes 2097168 | tf_op jit(solution)/shard_map/all_gather | solution.py:86
  64.2 61.5 %while.52 = (s32[]{:T(128)}, f32[1,256,512]{2,1,0:T(8,128)S(1)}, f32[1,256]{1,0:T(1,128)S(1)}, f32[8,64,1,512]{3,1,2,0:T(8,128)}, f32[8,1,256,512]{3,2,1,0:T(8,1...) while((s32[]{:T(128)}, f32[1,256,512]{2,1,0:T(8,128)S(1)}, ...), condition=%wide.region_9.10_spmd.clone, body=%wide.region_7.9_spmd.clone.sunk | while | flops 27890436 | bytes 12177578 | solution.py:126
  126.6 613.5 %while.51 = (s32[]{:T(128)}, f32[1,256,512]{2,1,0:T(8,128)}, f32[1,256,512]{2,1,0:T(8,128)}, pred[]{:T(512)}, f32[1,256]{1,0:T(1,128)S(1)}, /*index=5*/f32[1,256,512]{2,1,0:T(8,128)S(1)}, s32[]{:T(128)}) while((s32[]{:T(128)}, f32[1,256,512]{2,1,0:T(8,128)}, f32[1,256,512]{2,1,0:T(8,128)}, pred[]{:T(512)}, f32[1,256]{1,0:T(1,128)S(1)}, ...), condition=%wide.region_11.12_spmd, body=%wide.region_10.11_spmd.sunk | while | flops 393218 | bytes 4195446 | solution.py:145
  128.6 6.4 collective-permute-done
  140.4 6.4 collective-permute-done
  152.2 6.4 collective-permute-done
  164.0 6.4 collective-permute-done
  175.8 6.4 collective-permute-done
  187.6 6.4 collective-permute-done
  199.4 6.4 collective-permute-done
  211.2 6.4 collective-permute-done
  223.0 6.4 collective-permute-done
  234.8 6.4 collective-permute-done
  246.7 6.4 collective-permute-done
  258.5 6.4 collective-permute-done
  270.3 6.4 collective-permute-done
  282.1 6.4 collective-permute-done
  293.9 6.4 collective-permute-done
  305.7 6.4 collective-permute-done
  317.5 6.4 collective-permute-done
  329.3 6.4 collective-permute-done
  342.9 6.4 collective-permute-done
  356.9 6.4 collective-permute-done
  364.4 6.4 collective-permute-start
  370.8 6.4 collective-permute-done
  378.3 6.4 collective-permute-start
  384.7 6.4 collective-permute-done
  398.6 6.4 collective-permute-done
  412.5 6.4 collective-permute-done
  420.0 6.4 collective-permute-start
  426.4 6.4 collective-permute-done
  440.3 6.4 collective-permute-done
  454.2 6.4 collective-permute-done
  468.2 6.4 collective-permute-done
  475.7 6.4 collective-permute-start
  482.1 6.4 collective-permute-done
  496.0 6.4 collective-permute-done
  509.9 6.4 collective-permute-done
  523.8 6.4 collective-permute-done
  531.3 6.4 collective-permute-start
  537.7 6.4 collective-permute-done
  551.6 6.4 collective-permute-done
  565.5 6.4 collective-permute-done
  579.5 6.4 collective-permute-done
  593.4 6.4 collective-permute-done
  607.3 6.4 collective-permute-done
  621.2 6.4 collective-permute-done
  635.1 6.4 collective-permute-done
  649.0 6.4 collective-permute-done
  662.9 6.4 collective-permute-done
  676.8 6.4 collective-permute-done
  690.8 6.4 collective-permute-done
  704.7 6.4 collective-permute-done
  718.6 6.4 collective-permute-done
  732.5 6.4 collective-permute-done
  748.9 640.3 %while.53 = (s32[]{:T(128)}, f32[2,1,256,512]{3,2,1,0:T(8,128)S(1)}, bf16[2,3,1,1024]{3,2,1,0:T(2,128)(2,1)S(1)}, s32[2]{0:T(128)S(1)}, s32[3]{0:T(128)S(1)}, /*...) while((s32[]{:T(128)}, ...), condition=%wide.region_18.19_spmd.clone, body=%wide.region_14.18_spmd.clone.sunk | while | flops 935956 | bytes 5560569 | solution.py:192
  750.9 160.4 %psum.41 = bf16[3,1024]{1,0:T(4,128)(2,1)S(1)} all-reduce(bf16[3,1024]{1,0:T(4,128)(2,1)S(1)} %select_bitcast_fusion.5), channel_id=1, replica_groups=mesh['seq'=64,'tensor'=4] {'seq'}, use_global_device_ids=true, to_apply=%region_17.17 | all-reduce | flops 3072 | bytes 12288 | tf_op jit(solution)/shard_map/while/body/eval_jaxpr/psum | solution.py:20
  911.5 114.8 %all-reduce.2.cloned.1.call-done = bf16[256,512]{1,0:T(8,128)(2,1)} async-done(((bf16[256,512]{1,0:T(8,128)(2,1)}), bf16[256,512]{1,0:T(8,128)(2,1)}) %all-reduce.2.cloned.1.call-update) | async-done | bytes 262160 | tf_op jit(solution)/shard_map/while/body/eval_jaxpr/psum | solution.py:20
  1029.7 124.7 %psum.41 = bf16[3,1024]{1,0:T(4,128)(2,1)S(1)} all-reduce(bf16[3,1024]{1,0:T(4,128)(2,1)S(1)} %select_bitcast_fusion.5), channel_id=1, replica_groups=mesh['seq'=64,'tensor'=4] {'seq'}, use_global_device_ids=true, to_apply=%region_17.17 | all-reduce | flops 3072 | bytes 12288 | tf_op jit(solution)/shard_map/while/body/eval_jaxpr/psum | solution.py:20
  1154.5 52.8 %all-reduce.2.cloned.1.call-done = bf16[256,512]{1,0:T(8,128)(2,1)} async-done(((bf16[256,512]{1,0:T(8,128)(2,1)}), bf16[256,512]{1,0:T(8,128)(2,1)}) %all-reduce.2.cloned.1.call-update) | async-done | bytes 262160 | tf_op jit(solution)/shard_map/while/body/eval_jaxpr/psum | solution.py:20
  1210.7 124.6 %psum.41 = bf16[3,1024]{1,0:T(4,128)(2,1)S(1)} all-reduce(bf16[3,1024]{1,0:T(4,128)(2,1)S(1)} %select_bitcast_fusion.5), channel_id=1, replica_groups=mesh['seq'=64,'tensor'=4] {'seq'}, use_global_device_ids=true, to_apply=%region_17.17 | all-reduce | flops 3072 | bytes 12288 | tf_op jit(solution)/shard_map/while/body/eval_jaxpr/psum | solution.py:20
  1335.4 52.5 %all-reduce.2.cloned.1.call-done = bf16[256,512]{1,0:T(8,128)(2,1)} async-done(((bf16[256,512]{1,0:T(8,128)(2,1)}), bf16[256,512]{1,0:T(8,128)(2,1)}) %all-reduce.2.cloned.1.call-update) | async-done | bytes 262160 | tf_op jit(solution)/shard_map/while/body/eval_jaxpr/psum | solution.py:20
  1390.4 31.2 %reduce-scatter.2.cloned.1.call-done = bf16[128,2048]{1,0:T(8,128)(2,1)} async-done(((bf16[512,2048]{1,0:T(8,128)(2,1)}), bf16[128,2048]{1,0:T(8,128)(2,1)}) %reduce-scatter.2.cloned.1.call-update) | async-done | bytes 524304 | tf_op jit(solution)/shard_map/reduce_scatter | solution.py:164
  (338 shorter events, 385.0 us)
Async XLA Ops:
  7.2 739.0 %copy-start = (bf16[512,2048]{1,0:T(8,128)(2,1)S(1)}, bf16[512,2048]{1,0:T(8,128)(2,1)}, u32[]{:S(2)}) copy-start(bf16[512,2048]{1,0:T(8,128)(2,1)} %param.28) | copy-start | bytes 6291460
  7.2 39.6 %all-gather.2.cloned.1.call-start = ((), (), s32[]{:S(2)}) async-start(), calls=%async_computation.1 | async-start | bytes 2621440 | tf_op jit(solution)/shard_map/all_gather | solution.py:86
  24.7 31.7 %copy-start.13 = (f32[2048]{0:T(1024)S(1)}, f32[2048]{0:T(1024)}, u32[]{:S(2)}) copy-start(f32[2048]{0:T(1024)} %param.20) | copy-start | bytes 24580
  46.8 9.6 copy-start.9
  46.8 9.6 copy-start.10
  52.1 8.8 copy-start.3
  52.2 6.3 copy-start.11
  52.2 8.7 collective-permute-start.1
  126.5 613.5 %copy-start.7 = (bf16[8,64,1,256]{3,1,2,0:T(8,128)(2,1)S(1)}, bf16[8,64,1,256]{3,1,2,0:T(8,128)(2,1)}, u32[]{:S(2)}) copy-start(bf16[8,64,1,256]{3,1,2,0:T(8,128)(2,1)} %get-tuple-element.282) | copy-start | bytes 786436
  126.6 8.5 collective-permute-start
  136.1 10.7 collective-permute-start
  148.0 10.7 collective-permute-start
  159.8 10.7 collective-permute-start
  171.6 10.7 collective-permute-start
  183.4 10.7 collective-permute-start
  195.2 10.7 collective-permute-start
  207.0 10.7 collective-permute-start
  218.8 10.7 collective-permute-start
  230.6 10.7 collective-permute-start
  242.4 10.7 collective-permute-start
  254.2 10.7 collective-permute-start
  266.0 10.7 collective-permute-start
  277.8 10.7 collective-permute-start
  289.6 10.7 collective-permute-start
  301.4 10.7 collective-permute-start
  313.2 10.7 collective-permute-start
  325.0 10.7 collective-permute-start
  336.8 12.6 collective-permute-start
  350.5 12.8 collective-permute-start
  364.4 12.8 collective-permute-start
  378.3 12.8 collective-permute-start
  392.2 12.8 collective-permute-start
  406.1 12.8 collective-permute-start
  420.0 12.8 collective-permute-start
  433.9 12.8 collective-permute-start
  447.9 12.8 collective-permute-start
  461.8 12.8 collective-permute-start
  475.7 12.8 collective-permute-start
  489.6 12.8 collective-permute-start
  503.5 12.8 collective-permute-start
  517.4 12.8 collective-permute-start
  531.3 12.8 collective-permute-start
  545.2 12.8 collective-permute-start
  559.2 12.8 collective-permute-start
  573.1 12.8 collective-permute-start
  587.0 12.8 collective-permute-start
  600.9 12.8 collective-permute-start
  614.8 12.8 collective-permute-start
  628.7 12.8 collective-permute-start
  642.6 12.8 collective-permute-start
  656.5 12.8 collective-permute-start
  670.4 12.8 collective-permute-start
  684.4 12.8 collective-permute-start
  698.3 12.8 collective-permute-start
  712.2 12.8 collective-permute-start
  726.1 12.8 collective-permute-start
  740.0 4.5 copy-start.5
  746.2 2.6 copy-start.1
  746.2 2.6 copy-start.15
  748.9 277.5 %all-reduce.2.cloned.1.call-start = ((), (), s32[]{:S(2)}) async-start(), calls=%async_computation.3 | async-start | bytes 524288 | tf_op jit(solution)/shard_map/while/body/eval_jaxpr/psum | solution.py:20
  1027.6 179.7 %all-reduce.2.cloned.1.call-start = ((), (), s32[]{:S(2)}) async-start(), calls=%async_computation.3 | async-start | bytes 524288 | tf_op jit(solution)/shard_map/while/body/eval_jaxpr/psum | solution.py:20
  1208.6 179.3 %all-reduce.2.cloned.1.call-start = ((), (), s32[]{:S(2)}) async-start(), calls=%async_computation.3 | async-start | bytes 524288 | tf_op jit(solution)/shard_map/while/body/eval_jaxpr/psum | solution.py:20
  1389.2 34.4 %copy-start.2 = (f32[2,1,256,512]{3,2,1,0:T(8,128)}, f32[2,1,256,512]{3,2,1,0:T(8,128)S(1)}, u32[]{:S(2)}) copy-start(f32[2,1,256,512]{3,2,1,0:T(8,128)S(1)} %get-tuple-element.275) | copy-start | bytes 3145732
  1389.2 32.4 %reduce-scatter.2.cloned.1.call-start = ((), (), s32[]{:S(2)}) async-start(), calls=%async_computation.2 | async-start | bytes 2621440 | tf_op jit(solution)/shard_map/reduce_scatter | solution.py:164
  (5 other events, 5.2 us)
Sparse Core Ops, SparseCore 0:
  9.8 36.9 all-gather.1
  753.7 272.5 all-reduce.1
  1032.5 174.7 all-reduce.1
  1213.1 174.7 all-reduce.1
  1392.3 29.2 reduce-scatter.1
where the time goes:
time: 1430 us
  waiting for transfers between devices  576 us (40%)
  blocking collectives  419 us (29%)
  starting transfers between devices  264 us (18%)
  other arithmetic  105 us (7%)
  matrix products  25.5 us (2%)
  local copies, waits for them, and re-layouts  21.7 us (2%)
  between operations  15.9 us (1%)
    psum x3, blocking collectives, broadcast(): return lax.psum(block, axis)  410 us
    ppermute x48, waiting for transfers between devices, from_behind(): return lax.ppermute(array, axis, pairs)  302 us
    ppermute x48, starting transfers between devices, from_behind(): return lax.ppermute(array, axis, pairs)  264 us
    psum x3, waiting for transfers between devices, broadcast(): return lax.psum(block, axis)  220 us
    add x47, other arithmetic, relay(): return (received, decay_total[:, :, None] * received + local_state)  51.8 us
    reduce_scatter x1, waiting for transfers between devices, body(): lax.psum_scatter(jnp.dot(gated, w_out, preferred_element_type=jnp.float32...  31.2 us
  transfers between devices with their start and end apart: 53, of which 52 were waited for; matrix products, arithmetic and copies ran while one was open for 1% of the time, Pallas kernels for 0%

commit v1 on v0

--- a/solution.py
+++ b/solution.py
@@ -17,7 +17,7 @@
 
 def broadcast(block, axis, source):
     block = jnp.where(lax.axis_index(axis) == source, block, jnp.zeros_like(block))
-    return lax.psum(block, axis)
+    return jnp.sum(lax.all_gather(block, axis), axis=0)
 
 
 def block_pass(carry, pieces):

time: 1430 us -> 1220 us (0.85)
  blocking collectives: 419 us -> 253 us
  waiting for transfers between devices: 576 us -> 505 us
  other arithmetic: 105 us -> 135 us
    psum x3 -> x0, blocking collectives: 410 us -> none  [broadcast(): return lax.psum(block, axis)]
    all_gather x0 -> x3, blocking collectives: none -> 243 us  [broadcast(): return jnp.sum(lax.all_gather(block, axis), axis=0)]
    psum x3 -> x0, waiting for transfers between devices: 220 us -> none  [broadcast(): return lax.psum(block, axis)]
    all_gather x0 -> x3, waiting for transfers between devices: none -> 149 us  [broadcast(): return jnp.sum(lax.all_gather(block, axis), axis=0)]
    reduce_sum x0 -> x6, other arithmetic: none -> 27.2 us  [broadcast(): return jnp.sum(lax.all_gather(block, axis), axis=0)]
where the time goes in v1:
time: 1220 us
  waiting for transfers between devices  505 us (41%)
  starting transfers between devices  264 us (22%)
  blocking collectives  253 us (21%)
  other arithmetic  135 us (11%)
  matrix products  25.5 us (2%)
  local copies, waits for them, and re-layouts  21.7 us (2%)
  between operations  15.8 us (1%)
    ppermute x48, waiting for transfers between devices, from_behind(): return lax.ppermute(array, axis, pairs)  302 us
    ppermute x48, starting transfers between devices, from_behind(): return lax.ppermute(array, axis, pairs)  263 us
    all_gather x3, blocking collectives, broadcast(): return jnp.sum(lax.all_gather(block, axis), axis=0)  243 us
    all_gather x3, waiting for transfers between devices, broadcast(): return jnp.sum(lax.all_gather(block, axis), axis=0)  149 us
    add x47, other arithmetic, relay(): return (received, decay_total[:, :, None] * received + local_state)  51.8 us
    reduce_scatter x1, waiting for transfers between devices, body(): lax.psum_scatter(jnp.dot(gated, w_out, preferred_element_type=jnp.float32...  30.6 us
    reduce_sum x6, other arithmetic, broadcast(): return jnp.sum(lax.all_gather(block, axis), axis=0)  27.2 us
  transfers between devices with their start and end apart: 53, of which 52 were waited for; matrix products, arithmetic and copies ran while one was open for 1% of the time, Pallas kernels for 0%

profile of v1, /device:TPU:1, one launch (start us, length us, event | category | flops | bytes accessed | tf_op | source)
XLA Modules:
  0.0 1221.6 jit_solution(18345712619564535556)
XLA Ops:
  14.5 9.3 psum.7
  24.5 22.2 %all-gather.3.cloned.1.call-done = bf16[512,2048]{1,0:T(8,128)(2,1)} async-done(((bf16[512,512]{1,0:T(8,128)(2,1)}), bf16[512,2048]{1,0:T(8,128)(2,1)}) %all-gather.3.cloned.1.call-update) | async-done | bytes 2097168 | tf_op jit(solution)/shard_map/all_gather | solution.py:86
  64.2 61.5 %while.53 = (s32[]{:T(128)}, f32[1,256,512]{2,1,0:T(8,128)S(1)}, f32[1,256]{1,0:T(1,128)S(1)}, f32[8,64,1,512]{3,1,2,0:T(8,128)}, f32[8,1,256,512]{3,2,1,0:T(8,1...) while((s32[]{:T(128)}, f32[1,256,512]{2,1,0:T(8,128)S(1)}, ...), condition=%wide.region_9.10_spmd.clone, body=%wide.region_7.9_spmd.clone.sunk | while | flops 27890436 | bytes 12177578 | solution.py:126
  126.5 613.5 %while.52 = (s32[]{:T(128)}, f32[1,256,512]{2,1,0:T(8,128)}, f32[1,256,512]{2,1,0:T(8,128)}, pred[]{:T(512)}, f32[1,256]{1,0:T(1,128)S(1)}, /*index=5*/f32[1,256,512]{2,1,0:T(8,128)S(1)}, s32[]{:T(128)}) while((s32[]{:T(128)}, f32[1,256,512]{2,1,0:T(8,128)}, f32[1,256,512]{2,1,0:T(8,128)}, pred[]{:T(512)}, f32[1,256]{1,0:T(1,128)S(1)}, ...), condition=%wide.region_11.12_spmd, body=%wide.region_10.11_spmd.sunk | while | flops 393218 | bytes 4195446 | solution.py:145
  128.4 6.4 collective-permute-done
  140.2 6.4 collective-permute-done
  152.0 6.4 collective-permute-done
  163.8 6.4 collective-permute-done
  175.6 6.4 collective-permute-done
  187.4 6.4 collective-permute-done
  199.2 6.4 collective-permute-done
  211.0 6.4 collective-permute-done
  222.8 6.4 collective-permute-done
  234.6 6.4 collective-permute-done
  246.4 6.4 collective-permute-done
  258.2 6.4 collective-permute-done
  270.0 6.4 collective-permute-done
  281.9 6.4 collective-permute-done
  293.7 6.4 collective-permute-done
  305.5 6.4 collective-permute-done
  317.3 6.4 collective-permute-done
  329.1 6.4 collective-permute-done
  342.9 6.4 collective-permute-done
  356.8 6.4 collective-permute-done
  364.4 6.4 collective-permute-start
  370.7 6.4 collective-permute-done
  384.7 6.4 collective-permute-done
  398.6 6.4 collective-permute-done
  412.5 6.4 collective-permute-done
  420.0 6.4 collective-permute-start
  426.4 6.4 collective-permute-done
  440.3 6.4 collective-permute-done
  454.2 6.4 collective-permute-done
  468.1 6.4 collective-permute-done
  482.0 6.4 collective-permute-done
  495.9 6.4 collective-permute-done
  509.9 6.4 collective-permute-done
  523.8 6.4 collective-permute-done
  537.7 6.4 collective-permute-done
  551.6 6.4 collective-permute-done
  565.5 6.4 collective-permute-done
  579.4 6.4 collective-permute-done
  593.3 6.4 collective-permute-done
  607.2 6.4 collective-permute-done
  621.2 6.4 collective-permute-done
  635.1 6.4 collective-permute-done
  649.0 6.4 collective-permute-done
  662.9 6.4 collective-permute-done
  676.8 6.4 collective-permute-done
  690.7 6.4 collective-permute-done
  704.6 6.4 collective-permute-done
  718.5 6.4 collective-permute-done
  732.5 6.4 collective-permute-done
  748.9 432.4 %while.54 = (s32[]{:T(128)}, f32[2,1,256,512]{3,2,1,0:T(8,128)}, bf16[2,3,1,1024]{3,2,1,0:T(2,128)(2,1)S(1)}, s32[2]{0:T(128)S(1)}, s32[3]{0:T(128)S(1)}, /*inde...) while((s32[]{:T(128)}, f32[2,1,256,512]{3,2,1,0:T(8,128)}, ...), condition=%wide.region_18.19_spmd.clone, body=%wide.region_14.18_spmd.clone.sunk | while | flops 9252884 | bytes 72931576 | solution.py:192
  751.0 146.1 %all_gather.37 = bf16[64,3,1,1024]{3,1,2,0:T(4,128)(2,1)S(1)} all-gather(bf16[1,3,1,1024]{3,1,2,0:T(4,128)(2,1)S(1)} %broadcast_select_fusion.12), channel_id=1, replica_groups=mesh['seq'=64,'tensor'=4] {'seq'}, dimensions={0}, use_global_device_ids=true | all-gather | bytes 399360 | tf_op jit(solution)/shard_map/while/body/eval_jaxpr/all_gather | solution.py:20
  897.4 50.5 %all-gather.5.cloned.1.call-done = bf16[64,1,256,512]{3,2,1,0:T(8,128)(2,1)} async-done(((bf16[1,1,256,512]{3,2,1,0:T(8,128)(2,1)}), bf16[64,1,256,512]{3,2,1,0:T(8,128)(2,1)}) %all-gather.5.cloned.1.call-update) | async-done | bytes 16777232 | tf_op jit(solution)/shard_map/while/body/eval_jaxpr/all_gather | solution.py:20
  947.8 8.8 reduce_sum.119
  960.0 48.6 %all_gather.37 = bf16[64,3,1,1024]{3,1,2,0:T(4,128)(2,1)S(1)} all-gather(bf16[1,3,1,1024]{3,1,2,0:T(4,128)(2,1)S(1)} %broadcast_select_fusion.12), channel_id=1, replica_groups=mesh['seq'=64,'tensor'=4] {'seq'}, dimensions={0}, use_global_device_ids=true | all-gather | bytes 399360 | tf_op jit(solution)/shard_map/while/body/eval_jaxpr/all_gather | solution.py:20
  1009.0 49.4 %all-gather.5.cloned.1.call-done = bf16[64,1,256,512]{3,2,1,0:T(8,128)(2,1)} async-done(((bf16[1,1,256,512]{3,2,1,0:T(8,128)(2,1)}), bf16[64,1,256,512]{3,2,1,0:T(8,128)(2,1)}) %all-gather.5.cloned.1.call-update) | async-done | bytes 16777232 | tf_op jit(solution)/shard_map/while/body/eval_jaxpr/all_gather | solution.py:20
  1058.4 8.8 reduce_sum.119
  1071.8 48.6 %all_gather.37 = bf16[64,3,1,1024]{3,1,2,0:T(4,128)(2,1)S(1)} all-gather(bf16[1,3,1,1024]{3,1,2,0:T(4,128)(2,1)S(1)} %broadcast_select_fusion.12), channel_id=1, replica_groups=mesh['seq'=64,'tensor'=4] {'seq'}, dimensions={0}, use_global_device_ids=true | all-gather | bytes 399360 | tf_op jit(solution)/shard_map/while/body/eval_jaxpr/all_gather | solution.py:20
  1120.8 49.1 %all-gather.5.cloned.1.call-done = bf16[64,1,256,512]{3,2,1,0:T(8,128)(2,1)} async-done(((bf16[1,1,256,512]{3,2,1,0:T(8,128)(2,1)}), bf16[64,1,256,512]{3,2,1,0:T(8,128)(2,1)}) %all-gather.5.cloned.1.call-update) | async-done | bytes 16777232 | tf_op jit(solution)/shard_map/while/body/eval_jaxpr/all_gather | solution.py:20
  1169.9 8.8 reduce_sum.119
  1182.5 30.6 %reduce-scatter.2.cloned.1.call-done = bf16[128,2048]{1,0:T(8,128)(2,1)} async-done(((bf16[512,2048]{1,0:T(8,128)(2,1)}), bf16[128,2048]{1,0:T(8,128)(2,1)}) %reduce-scatter.2.cloned.1.call-update) | async-done | bytes 524304 | tf_op jit(solution)/shard_map/reduce_scatter | solution.py:164
  (338 shorter events, 407.4 us)
Async XLA Ops:
  7.2 739.1 %copy-start = (bf16[512,2048]{1,0:T(8,128)(2,1)S(1)}, bf16[512,2048]{1,0:T(8,128)(2,1)}, u32[]{:S(2)}) copy-start(bf16[512,2048]{1,0:T(8,128)(2,1)} %param.28) | copy-start | bytes 6291460
  7.2 39.6 %all-gather.3.cloned.1.call-start = ((), (), s32[]{:S(2)}) async-start(), calls=%async_computation.1 | async-start | bytes 2621440 | tf_op jit(solution)/shard_map/all_gather | solution.py:86
  24.5 31.6 %copy-start.10 = (f32[2048]{0:T(1024)S(1)}, f32[2048]{0:T(1024)}, u32[]{:S(2)}) copy-start(f32[2048]{0:T(1024)} %param.20) | copy-start | bytes 24580
  46.8 9.4 copy-start.6
  46.8 9.4 copy-start.7
  52.1 8.6 copy-start.1
  52.2 6.1 copy-start.8
  52.2 8.6 collective-permute-start.1
  126.5 8.3 collective-permute-start
  135.9 10.7 collective-permute-start
  147.7 10.7 collective-permute-start
  159.5 10.7 collective-permute-start
  171.3 10.7 collective-permute-start
  183.2 10.7 collective-permute-start
  195.0 10.7 collective-permute-start
  206.8 10.7 collective-permute-start
  218.6 10.7 collective-permute-start
  230.4 10.7 collective-permute-start
  242.2 10.7 collective-permute-start
  254.0 10.7 collective-permute-start
  265.8 10.7 collective-permute-start
  277.6 10.7 collective-permute-start
  289.4 10.7 collective-permute-start
  301.2 10.7 collective-permute-start
  313.0 10.7 collective-permute-start
  324.8 10.7 collective-permute-start
  336.6 12.7 %collective-permute-start = (f32[1,256,512]{2,1,0:T(8,128)}, f32[1,256,512]{2,1,0:T(8,128)S(1)}, u32[]{:S(2)}, u32[]{:S(2)}) collective-permute-start(f32[1,256,512]{2,1,0:T(8,128)} %get-tuple-element.692), channel_id=1, source_target_pairs={{0,4},{4,8},{8,12},{12,16},{16,20},{20,24},{24,28},{28,32},{32,36}... | collective-permute-start | bytes 1572872 | tf_op jit(solution)/shard_map/while/body/eval_jaxpr/ppermute | solution.py:15
  350.4 12.8 %collective-permute-start = (f32[1,256,512]{2,1,0:T(8,128)}, f32[1,256,512]{2,1,0:T(8,128)S(1)}, u32[]{:S(2)}, u32[]{:S(2)}) collective-permute-start(f32[1,256,512]{2,1,0:T(8,128)} %get-tuple-element.692), channel_id=1, source_target_pairs={{0,4},{4,8},{8,12},{12,16},{16,20},{20,24},{24,28},{28,32},{32,36}... | collective-permute-start | bytes 1572872 | tf_op jit(solution)/shard_map/while/body/eval_jaxpr/ppermute | solution.py:15
  364.4 12.8 %collective-permute-start = (f32[1,256,512]{2,1,0:T(8,128)}, f32[1,256,512]{2,1,0:T(8,128)S(1)}, u32[]{:S(2)}, u32[]{:S(2)}) collective-permute-start(f32[1,256,512]{2,1,0:T(8,128)} %get-tuple-element.692), channel_id=1, source_target_pairs={{0,4},{4,8},{8,12},{12,16},{16,20},{20,24},{24,28},{28,32},{32,36}... | collective-permute-start | bytes 1572872 | tf_op jit(solution)/shard_map/while/body/eval_jaxpr/ppermute | solution.py:15
  378.3 12.8 %collective-permute-start = (f32[1,256,512]{2,1,0:T(8,128)}, f32[1,256,512]{2,1,0:T(8,128)S(1)}, u32[]{:S(2)}, u32[]{:S(2)}) collective-permute-start(f32[1,256,512]{2,1,0:T(8,128)} %get-tuple-element.692), channel_id=1, source_target_pairs={{0,4},{4,8},{8,12},{12,16},{16,20},{20,24},{24,28},{28,32},{32,36}... | collective-permute-start | bytes 1572872 | tf_op jit(solution)/shard_map/while/body/eval_jaxpr/ppermute | solution.py:15
  392.2 12.8 %collective-permute-start = (f32[1,256,512]{2,1,0:T(8,128)}, f32[1,256,512]{2,1,0:T(8,128)S(1)}, u32[]{:S(2)}, u32[]{:S(2)}) collective-permute-start(f32[1,256,512]{2,1,0:T(8,128)} %get-tuple-element.692), channel_id=1, source_target_pairs={{0,4},{4,8},{8,12},{12,16},{16,20},{20,24},{24,28},{28,32},{32,36}... | collective-permute-start | bytes 1572872 | tf_op jit(solution)/shard_map/while/body/eval_jaxpr/ppermute | solution.py:15
  406.1 12.8 %collective-permute-start = (f32[1,256,512]{2,1,0:T(8,128)}, f32[1,256,512]{2,1,0:T(8,128)S(1)}, u32[]{:S(2)}, u32[]{:S(2)}) collective-permute-start(f32[1,256,512]{2,1,0:T(8,128)} %get-tuple-element.692), channel_id=1, source_target_pairs={{0,4},{4,8},{8,12},{12,16},{16,20},{20,24},{24,28},{28,32},{32,36}... | collective-permute-start | bytes 1572872 | tf_op jit(solution)/shard_map/while/body/eval_jaxpr/ppermute | solution.py:15
  420.0 12.8 %collective-permute-start = (f32[1,256,512]{2,1,0:T(8,128)}, f32[1,256,512]{2,1,0:T(8,128)S(1)}, u32[]{:S(2)}, u32[]{:S(2)}) collective-permute-start(f32[1,256,512]{2,1,0:T(8,128)} %get-tuple-element.692), channel_id=1, source_target_pairs={{0,4},{4,8},{8,12},{12,16},{16,20},{20,24},{24,28},{28,32},{32,36}... | collective-permute-start | bytes 1572872 | tf_op jit(solution)/shard_map/while/body/eval_jaxpr/ppermute | solution.py:15
  433.9 12.8 %collective-permute-start = (f32[1,256,512]{2,1,0:T(8,128)}, f32[1,256,512]{2,1,0:T(8,128)S(1)}, u32[]{:S(2)}, u32[]{:S(2)}) collective-permute-start(f32[1,256,512]{2,1,0:T(8,128)} %get-tuple-element.692), channel_id=1, source_target_pairs={{0,4},{4,8},{8,12},{12,16},{16,20},{20,24},{24,28},{28,32},{32,36}... | collective-permute-start | bytes 1572872 | tf_op jit(solution)/shard_map/while/body/eval_jaxpr/ppermute | solution.py:15
  447.8 12.8 %collective-permute-start = (f32[1,256,512]{2,1,0:T(8,128)}, f32[1,256,512]{2,1,0:T(8,128)S(1)}, u32[]{:S(2)}, u32[]{:S(2)}) collective-permute-start(f32[1,256,512]{2,1,0:T(8,128)} %get-tuple-element.692), channel_id=1, source_target_pairs={{0,4},{4,8},{8,12},{12,16},{16,20},{20,24},{24,28},{28,32},{32,36}... | collective-permute-start | bytes 1572872 | tf_op jit(solution)/shard_map/while/body/eval_jaxpr/ppermute | solution.py:15
  461.7 12.8 %collective-permute-start = (f32[1,256,512]{2,1,0:T(8,128)}, f32[1,256,512]{2,1,0:T(8,128)S(1)}, u32[]{:S(2)}, u32[]{:S(2)}) collective-permute-start(f32[1,256,512]{2,1,0:T(8,128)} %get-tuple-element.692), channel_id=1, source_target_pairs={{0,4},{4,8},{8,12},{12,16},{16,20},{20,24},{24,28},{28,32},{32,36}... | collective-permute-start | bytes 1572872 | tf_op jit(solution)/shard_map/while/body/eval_jaxpr/ppermute | solution.py:15
  475.6 12.8 %collective-permute-start = (f32[1,256,512]{2,1,0:T(8,128)}, f32[1,256,512]{2,1,0:T(8,128)S(1)}, u32[]{:S(2)}, u32[]{:S(2)}) collective-permute-start(f32[1,256,512]{2,1,0:T(8,128)} %get-tuple-element.692), channel_id=1, source_target_pairs={{0,4},{4,8},{8,12},{12,16},{16,20},{20,24},{24,28},{28,32},{32,36}... | collective-permute-start | bytes 1572872 | tf_op jit(solution)/shard_map/while/body/eval_jaxpr/ppermute | solution.py:15
  489.6 12.8 %collective-permute-start = (f32[1,256,512]{2,1,0:T(8,128)}, f32[1,256,512]{2,1,0:T(8,128)S(1)}, u32[]{:S(2)}, u32[]{:S(2)}) collective-permute-start(f32[1,256,512]{2,1,0:T(8,128)} %get-tuple-element.692), channel_id=1, source_target_pairs={{0,4},{4,8},{8,12},{12,16},{16,20},{20,24},{24,28},{28,32},{32,36}... | collective-permute-start | bytes 1572872 | tf_op jit(solution)/shard_map/while/body/eval_jaxpr/ppermute | solution.py:15
  503.5 12.8 %collective-permute-start = (f32[1,256,512]{2,1,0:T(8,128)}, f32[1,256,512]{2,1,0:T(8,128)S(1)}, u32[]{:S(2)}, u32[]{:S(2)}) collective-permute-start(f32[1,256,512]{2,1,0:T(8,128)} %get-tuple-element.692), channel_id=1, source_target_pairs={{0,4},{4,8},{8,12},{12,16},{16,20},{20,24},{24,28},{28,32},{32,36}... | collective-permute-start | bytes 1572872 | tf_op jit(solution)/shard_map/while/body/eval_jaxpr/ppermute | solution.py:15
  517.4 12.8 %collective-permute-start = (f32[1,256,512]{2,1,0:T(8,128)}, f32[1,256,512]{2,1,0:T(8,128)S(1)}, u32[]{:S(2)}, u32[]{:S(2)}) collective-permute-start(f32[1,256,512]{2,1,0:T(8,128)} %get-tuple-element.692), channel_id=1, source_target_pairs={{0,4},{4,8},{8,12},{12,16},{16,20},{20,24},{24,28},{28,32},{32,36}... | collective-permute-start | bytes 1572872 | tf_op jit(solution)/shard_map/while/body/eval_jaxpr/ppermute | solution.py:15
  531.3 12.8 %collective-permute-start = (f32[1,256,512]{2,1,0:T(8,128)}, f32[1,256,512]{2,1,0:T(8,128)S(1)}, u32[]{:S(2)}, u32[]{:S(2)}) collective-permute-start(f32[1,256,512]{2,1,0:T(8,128)} %get-tuple-element.692), channel_id=1, source_target_pairs={{0,4},{4,8},{8,12},{12,16},{16,20},{20,24},{24,28},{28,32},{32,36}... | collective-permute-start | bytes 1572872 | tf_op jit(solution)/shard_map/while/body/eval_jaxpr/ppermute | solution.py:15
  545.2 12.8 %collective-permute-start = (f32[1,256,512]{2,1,0:T(8,128)}, f32[1,256,512]{2,1,0:T(8,128)S(1)}, u32[]{:S(2)}, u32[]{:S(2)}) collective-permute-start(f32[1,256,512]{2,1,0:T(8,128)} %get-tuple-element.692), channel_id=1, source_target_pairs={{0,4},{4,8},{8,12},{12,16},{16,20},{20,24},{24,28},{28,32},{32,36}... | collective-permute-start | bytes 1572872 | tf_op jit(solution)/shard_map/while/body/eval_jaxpr/ppermute | solution.py:15
  559.1 12.8 %collective-permute-start = (f32[1,256,512]{2,1,0:T(8,128)}, f32[1,256,512]{2,1,0:T(8,128)S(1)}, u32[]{:S(2)}, u32[]{:S(2)}) collective-permute-start(f32[1,256,512]{2,1,0:T(8,128)} %get-tuple-element.692), channel_id=1, source_target_pairs={{0,4},{4,8},{8,12},{12,16},{16,20},{20,24},{24,28},{28,32},{32,36}... | collective-permute-start | bytes 1572872 | tf_op jit(solution)/shard_map/while/body/eval_jaxpr/ppermute | solution.py:15
  573.0 12.8 %collective-permute-start = (f32[1,256,512]{2,1,0:T(8,128)}, f32[1,256,512]{2,1,0:T(8,128)S(1)}, u32[]{:S(2)}, u32[]{:S(2)}) collective-permute-start(f32[1,256,512]{2,1,0:T(8,128)} %get-tuple-element.692), channel_id=1, source_target_pairs={{0,4},{4,8},{8,12},{12,16},{16,20},{20,24},{24,28},{28,32},{32,36}... | collective-permute-start | bytes 1572872 | tf_op jit(solution)/shard_map/while/body/eval_jaxpr/ppermute | solution.py:15
  586.9 12.8 %collective-permute-start = (f32[1,256,512]{2,1,0:T(8,128)}, f32[1,256,512]{2,1,0:T(8,128)S(1)}, u32[]{:S(2)}, u32[]{:S(2)}) collective-permute-start(f32[1,256,512]{2,1,0:T(8,128)} %get-tuple-element.692), channel_id=1, source_target_pairs={{0,4},{4,8},{8,12},{12,16},{16,20},{20,24},{24,28},{28,32},{32,36}... | collective-permute-start | bytes 1572872 | tf_op jit(solution)/shard_map/while/body/eval_jaxpr/ppermute | solution.py:15
  600.9 12.8 %collective-permute-start = (f32[1,256,512]{2,1,0:T(8,128)}, f32[1,256,512]{2,1,0:T(8,128)S(1)}, u32[]{:S(2)}, u32[]{:S(2)}) collective-permute-start(f32[1,256,512]{2,1,0:T(8,128)} %get-tuple-element.692), channel_id=1, source_target_pairs={{0,4},{4,8},{8,12},{12,16},{16,20},{20,24},{24,28},{28,32},{32,36}... | collective-permute-start | bytes 1572872 | tf_op jit(solution)/shard_map/while/body/eval_jaxpr/ppermute | solution.py:15
  614.8 12.8 %collective-permute-start = (f32[1,256,512]{2,1,0:T(8,128)}, f32[1,256,512]{2,1,0:T(8,128)S(1)}, u32[]{:S(2)}, u32[]{:S(2)}) collective-permute-start(f32[1,256,512]{2,1,0:T(8,128)} %get-tuple-element.692), channel_id=1, source_target_pairs={{0,4},{4,8},{8,12},{12,16},{16,20},{20,24},{24,28},{28,32},{32,36}... | collective-permute-start | bytes 1572872 | tf_op jit(solution)/shard_map/while/body/eval_jaxpr/ppermute | solution.py:15
  628.7 12.8 %collective-permute-start = (f32[1,256,512]{2,1,0:T(8,128)}, f32[1,256,512]{2,1,0:T(8,128)S(1)}, u32[]{:S(2)}, u32[]{:S(2)}) collective-permute-start(f32[1,256,512]{2,1,0:T(8,128)} %get-tuple-element.692), channel_id=1, source_target_pairs={{0,4},{4,8},{8,12},{12,16},{16,20},{20,24},{24,28},{28,32},{32,36}... | collective-permute-start | bytes 1572872 | tf_op jit(solution)/shard_map/while/body/eval_jaxpr/ppermute | solution.py:15
  642.6 12.8 %collective-permute-start = (f32[1,256,512]{2,1,0:T(8,128)}, f32[1,256,512]{2,1,0:T(8,128)S(1)}, u32[]{:S(2)}, u32[]{:S(2)}) collective-permute-start(f32[1,256,512]{2,1,0:T(8,128)} %get-tuple-element.692), channel_id=1, source_target_pairs={{0,4},{4,8},{8,12},{12,16},{16,20},{20,24},{24,28},{28,32},{32,36}... | collective-permute-start | bytes 1572872 | tf_op jit(solution)/shard_map/while/body/eval_jaxpr/ppermute | solution.py:15
  656.5 12.8 %collective-permute-start = (f32[1,256,512]{2,1,0:T(8,128)}, f32[1,256,512]{2,1,0:T(8,128)S(1)}, u32[]{:S(2)}, u32[]{:S(2)}) collective-permute-start(f32[1,256,512]{2,1,0:T(8,128)} %get-tuple-element.692), channel_id=1, source_target_pairs={{0,4},{4,8},{8,12},{12,16},{16,20},{20,24},{24,28},{28,32},{32,36}... | collective-permute-start | bytes 1572872 | tf_op jit(solution)/shard_map/while/body/eval_jaxpr/ppermute | solution.py:15
  670.4 12.8 %collective-permute-start = (f32[1,256,512]{2,1,0:T(8,128)}, f32[1,256,512]{2,1,0:T(8,128)S(1)}, u32[]{:S(2)}, u32[]{:S(2)}) collective-permute-start(f32[1,256,512]{2,1,0:T(8,128)} %get-tuple-element.692), channel_id=1, source_target_pairs={{0,4},{4,8},{8,12},{12,16},{16,20},{20,24},{24,28},{28,32},{32,36}... | collective-permute-start | bytes 1572872 | tf_op jit(solution)/shard_map/while/body/eval_jaxpr/ppermute | solution.py:15
  684.3 12.8 %collective-permute-start = (f32[1,256,512]{2,1,0:T(8,128)}, f32[1,256,512]{2,1,0:T(8,128)S(1)}, u32[]{:S(2)}, u32[]{:S(2)}) collective-permute-start(f32[1,256,512]{2,1,0:T(8,128)} %get-tuple-element.692), channel_id=1, source_target_pairs={{0,4},{4,8},{8,12},{12,16},{16,20},{20,24},{24,28},{28,32},{32,36}... | collective-permute-start | bytes 1572872 | tf_op jit(solution)/shard_map/while/body/eval_jaxpr/ppermute | solution.py:15
  698.2 12.8 %collective-permute-start = (f32[1,256,512]{2,1,0:T(8,128)}, f32[1,256,512]{2,1,0:T(8,128)S(1)}, u32[]{:S(2)}, u32[]{:S(2)}) collective-permute-start(f32[1,256,512]{2,1,0:T(8,128)} %get-tuple-element.692), channel_id=1, source_target_pairs={{0,4},{4,8},{8,12},{12,16},{16,20},{20,24},{24,28},{28,32},{32,36}... | collective-permute-start | bytes 1572872 | tf_op jit(solution)/shard_map/while/body/eval_jaxpr/ppermute | solution.py:15
  712.2 12.8 %collective-permute-start = (f32[1,256,512]{2,1,0:T(8,128)}, f32[1,256,512]{2,1,0:T(8,128)S(1)}, u32[]{:S(2)}, u32[]{:S(2)}) collective-permute-start(f32[1,256,512]{2,1,0:T(8,128)} %get-tuple-element.692), channel_id=1, source_target_pairs={{0,4},{4,8},{8,12},{12,16},{16,20},{20,24},{24,28},{28,32},{32,36}... | collective-permute-start | bytes 1572872 | tf_op jit(solution)/shard_map/while/body/eval_jaxpr/ppermute | solution.py:15
  726.1 12.8 %collective-permute-start = (f32[1,256,512]{2,1,0:T(8,128)}, f32[1,256,512]{2,1,0:T(8,128)S(1)}, u32[]{:S(2)}, u32[]{:S(2)}) collective-permute-start(f32[1,256,512]{2,1,0:T(8,128)} %get-tuple-element.692), channel_id=1, source_target_pairs={{0,4},{4,8},{8,12},{12,16},{16,20},{20,24},{24,28},{28,32},{32,36}... | collective-permute-start | bytes 1572872 | tf_op jit(solution)/shard_map/while/body/eval_jaxpr/ppermute | solution.py:15
  740.0 4.5 copy-start.3
  744.4 1.1 copy-start.5
  744.5 1.2 copy-start.2
  744.5 1.4 copy-start.4
  746.3 2.6 copy-start.12
  748.9 198.9 %all-gather.5.cloned.1.call-start = ((), (), s32[]{:S(2)}) async-start(), calls=%async_computation.3 | async-start | bytes 17039360 | tf_op jit(solution)/shard_map/while/body/eval_jaxpr/all_gather | solution.py:20
  958.0 100.4 %all-gather.5.cloned.1.call-start = ((), (), s32[]{:S(2)}) async-start(), calls=%async_computation.3 | async-start | bytes 17039360 | tf_op jit(solution)/shard_map/while/body/eval_jaxpr/all_gather | solution.py:20
  1069.8 100.1 %all-gather.5.cloned.1.call-start = ((), (), s32[]{:S(2)}) async-start(), calls=%async_computation.3 | async-start | bytes 17039360 | tf_op jit(solution)/shard_map/while/body/eval_jaxpr/all_gather | solution.py:20
  1181.3 31.8 %reduce-scatter.2.cloned.1.call-start = ((), (), s32[]{:S(2)}) async-start(), calls=%async_computation.2 | async-start | bytes 2621440 | tf_op jit(solution)/shard_map/reduce_scatter | solution.py:164
  (2 other events, 1.5 us)
Sparse Core Ops, SparseCore 0:
  9.8 36.9 all-gather.2
  753.0 194.7 all-gather.4
  962.1 96.2 all-gather.4
  1073.6 96.2 all-gather.4
  1184.3 28.7 reduce-scatter.1
